TPU v7x, 32 devices: a whole 2x2x4 slice. The times are simulated.
32 devices in a mesh: front: 4 (over y, core), row: 8 (over z, x).
Axes of the slice: x: 2, y: 2, z: 4, core: 2. Of those that a mesh axis runs over, the one named last changes fastest.
Arguments:
- rhs_diag: float32 [4, 32, 2048], P('front', None, 'row'), may hold values from -6 to 6
- rhs_off: float32 [4, 32, 12288], P('front', None, 'row'), may hold values from -6 to 6
- diag_factor: float32 [4, 2048, 2048], P('front', 'row'), may hold values from -0.125 to 0.125
- off_factor: float32 [4, 12288, 2048], P('front', 'row'), may hold values from -0.125 to 0.125
- diag_inverse: float32 [4, 4, 512, 512], P('front')
- pattern: int32 [4, 4, 96], P('front', None, 'row'), may hold values 0 or 1
- upd_vals: float32 [32, 4, 8, 4, 8, 128], P(None, 'front', 'row'), may hold values from -4 to 4
- upd_rows: int32 [4, 8, 4, 8, 128], P('front', 'row'), may hold values from 0 to 1791
Outputs:
- solved: float32 [4, 32, 2048], P('front', None, 'row')
- remainder: float32 [4, 32, 12288], P('front', None, 'row')
Inputs may be any that keep to these rules, and one draw needn't show every extreme that they name: `upd_rows`: relative rows of the receiving row block: below 256 a window row, else a row below the window; several entries may name one row.
All inputs are finite; a program needn't handle non-finite values. No bound on the sum of `pattern` on one device may be relied on, other than what follows from the above.
Results may differ from a plain program's by a relative error of at most 0.0001.
Values sent between devices are 32-bit elements; how exact they have to be, the bound alone decides.
A program may use at most 128 MiB of HBM per device.

v0:
```python
import jax
import jax.numpy as jnp
from jax import lax
from jax.sharding import PartitionSpec as P

W = 512
P_SIZE = 4
BR = 128


def local(rhs_diag, rhs_off, diag_factor, off_factor, diag_inverse, pattern, upd_vals, upd_rows):
    own_rows = diag_factor.shape[1]
    nrhs_count = upd_vals.shape[0]
    fronts_all = upd_vals.shape[3]
    groups_all = upd_vals.shape[4]
    slot_count = upd_vals.shape[5]
    flat_vals = upd_vals.reshape(nrhs_count, 1, fronts_all * groups_all, slot_count)
    arrived = lax.all_to_all(flat_vals, ("front", "row"), split_axis=2, concat_axis=1, tiled=True)
    received = arrived.reshape(nrhs_count, -1)
    targets = upd_rows.reshape(-1)
    combined = jnp.concatenate([rhs_diag[0], rhs_off[0]], axis=1)
    combined = combined.at[:, targets].add(received)
    upper = combined[:, :own_rows]
    lower = combined[:, own_rows:]
    diag_local = diag_factor[0]
    off_local = off_factor[0]
    inverse = diag_inverse[0]
    mask_rows = jnp.repeat(pattern[0].astype(jnp.float32), BR, axis=1)
    group = lax.axis_index("row")
    positions = group * own_rows + lax.iota(jnp.int32, own_rows)
    columns = lax.iota(jnp.int32, W)
    highest = lax.Precision.HIGHEST
    contract = (((1,), (1,)), ((), ()))
    pieces = []
    for panel in range(P_SIZE):
        picker = (
            (positions[:, None] // W == panel) & (positions[:, None] % W == columns[None, :])
        ).astype(jnp.float32)
        partial_rhs = jnp.dot(upper, picker, precision=highest, preferred_element_type=jnp.float32)
        panel_rhs = lax.psum(partial_rhs, "row")
        piece = lax.dot_general(
            panel_rhs,
            inverse[panel],
            contract,
            precision=highest,
            preferred_element_type=jnp.float32,
        )
        pieces.append(piece)
        upper = upper - lax.dot_general(
            piece,
            diag_local[:, panel * W : (panel + 1) * W],
            contract,
            precision=highest,
            preferred_element_type=jnp.float32,
        )
        term = lax.dot_general(
            piece,
            off_local[:, panel * W : (panel + 1) * W],
            contract,
            precision=highest,
            preferred_element_type=jnp.float32,
        )
        lower = lower - term * mask_rows[panel][None, :]
    solution = jnp.concatenate(pieces, axis=1)
    own_solution = lax.dynamic_slice_in_dim(solution, group * own_rows, own_rows, 1)
    return (own_solution[None], lower[None])


def solution(mesh):
    in_specs = (
        P("front", None, "row"),
        P("front", None, "row"),
        P("front", "row", None),
        P("front", "row", None),
        P("front", None, None, None),
        P("front", None, "row"),
        P(None, "front", "row", None, None, None),
        P("front", "row", None, None, None),
    )
    out_specs = (P("front", None, "row"), P("front", None, "row"))
    return jax.shard_map(local, mesh=mesh, in_specs=in_specs, out_specs=out_specs, check_vma=False)
```

profile of v0, /device:TPU:0, one launch (start us, length us, event | category | flops | bytes accessed | tf_op | source)
XLA Modules:
  0.0 367.9 jit_solution(12900171675111309321)
XLA Ops:
  7.2 2.1 copy.19
  9.3 7.3 %all-to-all-start = ((f32[32,1,32,128]{3,0,1,2:T(8,128)}), f32[32,1,32,128]{3,0,1,2:T(8,128)S(1)}, u32[]{:S(2)}, u32[]{:S(2)}) async-start(f32[32,1,32,128]{3,0,1,2:T(8,128)} %bitcast.4), calls=%async_computation | async-start | bytes 1048576 | tf_op jit(solution)/shard_map/all_to_all | solution.py:18
  16.7 0.5 broadcast_compare_fusion.2
  17.2 0.7 convert_element_type.3
  17.9 0.9 pad_maximum_fusion
  18.9 0.7 broadcast_bitcast_fusion
  19.5 0.7 broadcast_bitcast_fusion.2
  21.0 0.6 and_select_fusion
  21.6 0.7 compare_select_fusion
  22.3 10.5 %all-to-all-done = f32[32,1,32,128]{3,0,1,2:T(8,128)S(1)} async-done(((f32[32,1,32,128]{3,0,1,2:T(8,128)}), f32[32,1,32,128]{3,0,1,2:T(8,128)S(1)}, u32[]{:S(2)}, u32[]{:S(2)}) %all-to-all-start) | async-done | bytes 524320 | tf_op jit(solution)/shard_map/all_to_all | solution.py:18
  33.5 0.6 copy.22
  34.1 22.7 %scatter_fusion = f32[32,1792]{0,1:T(8,128)S(1)} fusion(f32[32,1792]{0,1:T(8,128)S(1)} %copy.21, s32[4096]{0:T(1024)S(1)} %bitcast.72, f32[4096,32]{1,0:T(8,128)S(1)} %copy.22), kind=kCustom, calls=%fused_computation | custom fusion | flops 131072 | bytes 1589248 | tf_op jit(solution)/shard_map/scatter-add | solution.py:22
  56.9 1.0 fusion.54
  58.1 67.0 %all-reduce.5.cloned.1.call-done = f32[32,512]{1,0:T(8,128)} async-done(((f32[32,512]{1,0:T(8,128)}), f32[32,512]{1,0:T(8,128)}) %all-reduce.5.cloned.1.call-update) | async-done | bytes 65552 | tf_op jit(solution)/shard_map/psum | solution.py:40
  125.1 2.3 fusion.41
  127.4 1.6 convolution_subtract_fusion.2
  129.0 1.0 fusion.56
  130.4 69.0 %all-reduce.7.cloned.1.call-done = f32[32,512]{1,0:T(8,128)} async-done(((f32[32,512]{1,0:T(8,128)}), f32[32,512]{1,0:T(8,128)}) %all-reduce.7.cloned.1.call-update) | async-done | bytes 65552 | tf_op jit(solution)/shard_map/psum | solution.py:40
  199.4 2.3 fusion.39
  201.7 1.6 convolution_subtract_fusion.1
  203.4 1.0 fusion.58
  204.6 4.8 %fusion.23 = f32[32,1536]{1,0:T(8,128)S(1)} fusion(f32[32,512]{1,0:T(8,128)S(1)} %fusion.39, f32[1536,2048]{1,0:T(8,128)} %bitcast.62, f32[1536]{0:T(1024)S(1)} %copy-done.3), kind=kOutput, calls=%fused_computation.14 | convolution fusion | flops 302039040 | bytes 3414016 | tf_op jit(solution)/shard_map/dot_general | solution.py:56
  209.4 64.3 %all-reduce.9.cloned.1.call-done = f32[32,512]{1,0:T(8,128)} async-done(((f32[32,512]{1,0:T(8,128)}), f32[32,512]{1,0:T(8,128)}) %all-reduce.9.cloned.1.call-update) | async-done | bytes 65552 | tf_op jit(solution)/shard_map/psum | solution.py:40
  273.7 2.3 fusion.37
  276.1 1.6 convolution_subtract_fusion
  277.7 1.0 fusion.60
  278.7 4.8 %fusion.26 = f32[32,1536]{1,0:T(8,128)S(1)} fusion(f32[32,512]{1,0:T(8,128)S(1)} %fusion.37, f32[1536,2048]{1,0:T(8,128)} %bitcast.63, f32[1536]{0:T(1024)S(1)} %copy-done.2), kind=kOutput, calls=%fused_computation.15 | convolution fusion | flops 302039040 | bytes 3414016 | tf_op jit(solution)/shard_map/dot_general | solution.py:56
  283.5 64.5 %all-reduce.11.cloned.1.call-done = f32[32,512]{1,0:T(8,128)} async-done(((f32[32,512]{1,0:T(8,128)}), f32[32,512]{1,0:T(8,128)}) %all-reduce.11.cloned.1.call-update) | async-done | bytes 65552 | tf_op jit(solution)/shard_map/psum | solution.py:40
  348.1 2.3 fusion.35
  350.4 4.8 %fusion.29 = f32[32,1536]{1,0:T(8,128)S(1)} fusion(f32[32,512]{1,0:T(8,128)S(1)} %fusion.35, f32[1536,2048]{1,0:T(8,128)} %bitcast.64, f32[1536]{0:T(1024)S(1)} %copy-done.1), kind=kOutput, calls=%fused_computation.16 | convolution fusion | flops 302039040 | bytes 3414016 | tf_op jit(solution)/shard_map/dot_general | solution.py:56
  355.2 0.6 fusion.73
  355.8 5.5 %fusion.32 = f32[1,32,1536]{2,1,0:T(8,128)} fusion(f32[32,1536]{1,0:T(8,128)S(1)} %fusion.29, f32[32,1536]{1,0:T(8,128)S(1)} %fusion.26, f32[32,1536]{1,0:T(8,128)S(1)} %fusion.23, f32[32,1536]{1,0:T(8,128)S(1)} %copy.26, f32[32,512]{1,0:T(8,128)S(1)} %fusion.41, f32[1536,2048]{1,0:T(8,128)} %bitcast.65, f32[1536]{0:T(1024)S(1)} %copy-done), kind=kOutput, calls=%fused_computation.17 | convolution fusion | flops 302235648 | bytes 4200448 | tf_op jit(solution)/shard_map/dot_general | solution.py:56
  (35 shorter events, 2.2 us)
Async XLA Ops:
  9.3 23.6 %all-to-all-start = ((f32[32,1,32,128]{3,0,1,2:T(8,128)}), f32[32,1,32,128]{3,0,1,2:T(8,128)S(1)}, u32[]{:S(2)}, u32[]{:S(2)}) async-start(f32[32,1,32,128]{3,0,1,2:T(8,128)} %bitcast.4), calls=%async_computation | async-start | bytes 1048576 | tf_op jit(solution)/shard_map/all_to_all | solution.py:18
  16.6 108.5 %all-reduce.5.cloned.1.call-start = ((), (), s32[]{:S(2)}) async-start(), calls=%async_computation.1 | async-start | bytes 131072 | tf_op jit(solution)/shard_map/psum | solution.py:40
  34.1 22.8 %copy-start.4 = (s32[256]{0:T(256)S(1)}, s32[256]{0:T(256)}, u32[]{:S(2)}) copy-start(s32[256]{0:T(256)} %and_select_fusion) | copy-start | bytes 3076
  34.1 22.8 %copy-start.7 = (pred[256]{0:T(512)(128)(4,1)S(1)}, pred[256]{0:T(512)(128)(4,1)}, u32[]{:S(2)}) copy-start(pred[256]{0:T(512)(128)(4,1)} %broadcast_compare_fusion.2) | copy-start | bytes 772
  34.1 94.9 %copy-start.6 = (pred[256]{0:T(512)(128)(4,1)S(1)}, pred[256]{0:T(512)(128)(4,1)}, u32[]{:S(2)}) copy-start(pred[256]{0:T(512)(128)(4,1)} %broadcast_compare_fusion.4) | copy-start | bytes 772
  56.9 146.5 %copy-start.5 = (s32[256]{0:T(256)S(1)}, s32[256]{0:T(256)}, u32[]{:S(2)}) copy-start(s32[256]{0:T(256)} %and_select_fusion) | copy-start | bytes 3076
  56.9 147.7 %copy-start.3 = (f32[1536]{0:T(1024)S(1)}, f32[1536]{0:T(1024)}, u32[]{:S(2)}) copy-start(f32[1536]{0:T(1024)} %get-tuple-element.8) | copy-start | bytes 18436
  57.9 141.5 %all-reduce.7.cloned.1.call-start = ((), (), s32[]{:S(2)}) async-start(), calls=%async_computation.2 | async-start | bytes 131072 | tf_op jit(solution)/shard_map/psum | solution.py:40
  130.1 143.7 %all-reduce.9.cloned.1.call-start = ((), (), s32[]{:S(2)}) async-start(), calls=%async_computation.3 | async-start | bytes 131072 | tf_op jit(solution)/shard_map/psum | solution.py:40
  130.2 148.5 %copy-start.2 = (f32[1536]{0:T(1024)S(1)}, f32[1536]{0:T(1024)}, u32[]{:S(2)}) copy-start(f32[1536]{0:T(1024)} %get-tuple-element.7) | copy-start | bytes 18436
  204.4 143.7 %all-reduce.11.cloned.1.call-start = ((), (), s32[]{:S(2)}) async-start(), calls=%async_computation.4 | async-start | bytes 131072 | tf_op jit(solution)/shard_map/psum | solution.py:40
  209.4 140.9 %copy-start.1 = (f32[1536]{0:T(1024)S(1)}, f32[1536]{0:T(1024)}, u32[]{:S(2)}) copy-start(f32[1536]{0:T(1024)} %get-tuple-element.6) | copy-start | bytes 18436
  278.7 77.2 %copy-start = (f32[1536]{0:T(1024)S(1)}, f32[1536]{0:T(1024)}, u32[]{:S(2)}) copy-start(f32[1536]{0:T(1024)} %get-tuple-element.9) | copy-start | bytes 18436
Sparse Core Ops, SparseCore 0:
  58.0 66.9 all-reduce.4
  130.2 69.1 all-reduce.6
  204.5 69.1 all-reduce.8
  278.8 69.1 all-reduce.10
where the time goes:
time: 369 us; the launch traced here: 368 us
  waiting for transfers between devices  275 us (75%)
  matrix products  37.9 us (10%)
  other arithmetic  27.4 us (7%)
  between operations  14 us (4%)
  starting transfers between devices  7.67 us (2%)
  local copies, waits for them, and re-layouts  5.4 us (1%)
    psum x4, waiting for transfers between devices, local(): panel_rhs = lax.psum(partial_rhs, 'row')  265 us
    scatter-add x1, other arithmetic, local(): combined = combined.at[:, targets].add(received)  22.7 us
    dot_general x4, matrix products, local(): lax.dot_general(piece, off_local[:, panel * W:(panel + 1) * W], contract,...  19.9 us
    all_to_all x1, waiting for transfers between devices, local(): lax.all_to_all(flat_vals, ('front', 'row'), split_axis=2, concat_axis=1,...  10.5 us
    dot_general x4, matrix products, local(): lax.dot_general(panel_rhs, inverse[panel], contract, precision=highest, p...  9.18 us
  transfers between devices with their start and end apart: 5, of which 5 were waited for; matrix products, arithmetic and copies ran while one was open for 4% of the time, Pallas kernels for 0%

commit v1 on v0

--- a/solution.py
+++ b/solution.py
@@ -37,7 +37,7 @@
             (positions[:, None] // W == panel) & (positions[:, None] % W == columns[None, :])
         ).astype(jnp.float32)
         partial_rhs = jnp.dot(upper, picker, precision=highest, preferred_element_type=jnp.float32)
-        panel_rhs = lax.psum(partial_rhs, "row")
+        panel_rhs = jnp.sum(lax.all_gather(partial_rhs, "row"), axis=0)
         piece = lax.dot_general(
             panel_rhs,
             inverse[panel],

time: 369 us -> 213 us (0.58)
  waiting for transfers between devices: 275 us -> 8.71 us
  blocking collectives: 0 us -> 125 us
  between operations: 14 us -> 0.92 us
    psum x4 -> x0, waiting for transfers between devices: 265 us -> none  [local(): panel_rhs = lax.psum(partial_rhs, 'row')]
    all_gather x0 -> x4, blocking collectives: none -> 125 us  [local(): panel_rhs = jnp.sum(lax.all_gather(partial_rhs, 'row'), axis=0)]
  transfers between devices with their start and end apart: 5 -> 1, of which waited for: 5 -> 1; matrix products, arithmetic and copies ran while one was open for 4% -> 4% of each run, Pallas kernels for 0% -> 0%
where the time goes in v1:
time: 213 us; the launch traced here: 212 us
  blocking collectives  125 us (59%)
  matrix products  35.3 us (17%)
  other arithmetic  28.7 us (13%)
  waiting for transfers between devices  8.71 us (4%)
  starting transfers between devices  7.33 us (3%)
  local copies, waits for them, and re-layouts  6.05 us (3%)
    all_gather x4, blocking collectives, local(): panel_rhs = jnp.sum(lax.all_gather(partial_rhs, 'row'), axis=0)  125 us
    scatter-add x1, other arithmetic, local(): combined = combined.at[:, targets].add(received)  22.7 us
    dot_general x4, matrix products, local(): lax.dot_general(piece, off_local[:, panel * W:(panel + 1) * W], contract,...  19.9 us
    dot_general x4, matrix products, local(): lax.dot_general(panel_rhs, inverse[panel], contract, precision=highest, p...  9.04 us
    all_to_all x1, waiting for transfers between devices, local(): lax.all_to_all(flat_vals, ('front', 'row'), split_axis=2, concat_axis=1,...  8.71 us
    all_to_all x1, starting transfers between devices, local(): lax.all_to_all(flat_vals, ('front', 'row'), split_axis=2, concat_axis=1,...  7.33 us
    dot_general x3, matrix products, local(): lax.dot_general(piece, diag_local[:, panel * W:(panel + 1) * W], contract...  4.84 us
  transfers between devices with their start and end apart: 1, of which 1 were waited for; matrix products, arithmetic and copies ran while one was open for 4% of the time, Pallas kernels for 0%

profile of v1, /device:TPU:0, one launch (start us, length us, event | category | flops | bytes accessed | tf_op | source)
XLA Modules:
  0.0 212.3 jit_solution(14548473937965722614)
XLA Ops:
  0.6 2.1 %copy.19 = f32[32,1,1,4,8,128]{5,0,4,3,2,1:T(8,128)} copy(f32[32,1,1,4,8,128]{5,4,3,2,1,0:T(8,128)} %param.14) | data formatting | bytes 1048576 | tf_op args[6]
  2.8 7.3 %all-to-all-start = ((f32[32,1,32,128]{3,0,1,2:T(8,128)}), f32[32,1,32,128]{3,0,1,2:T(8,128)S(1)}, u32[]{:S(2)}, u32[]{:S(2)}) async-start(f32[32,1,32,128]{3,0,1,2:T(8,128)} %bitcast.4), calls=%async_computation | async-start | bytes 1048576 | tf_op jit(solution)/shard_map/all_to_all | solution.py:18
  10.1 0.6 broadcast_compare_fusion.2
  10.7 0.5 broadcast_compare_fusion.4
  11.2 0.6 broadcast_compare_fusion.1
  11.8 0.7 convert_element_type.3
  12.5 0.7 broadcast_bitcast_fusion.2
  13.1 0.7 broadcast_bitcast_fusion.3
  13.8 0.9 pad_maximum_fusion
  14.7 0.7 broadcast_bitcast_fusion
  15.4 0.6 broadcast_compare_fusion
  16.3 0.6 and_select_fusion
  16.9 0.7 compare_select_fusion
  17.6 8.7 %all-to-all-done = f32[32,1,32,128]{3,0,1,2:T(8,128)S(1)} async-done(((f32[32,1,32,128]{3,0,1,2:T(8,128)}), f32[32,1,32,128]{3,0,1,2:T(8,128)S(1)}, u32[]{:S(2)}, u32[]{:S(2)}) %all-to-all-start) | async-done | bytes 524320 | tf_op jit(solution)/shard_map/all_to_all | solution.py:18
  27.0 0.6 copy.22
  27.6 22.7 %scatter_fusion = f32[32,1792]{0,1:T(8,128)S(1)} fusion(f32[32,1792]{0,1:T(8,128)S(1)} %copy.21, s32[4096]{0:T(1024)S(1)} %bitcast.80, f32[4096,32]{1,0:T(8,128)S(1)} %copy.22), kind=kCustom, calls=%fused_computation | custom fusion | flops 131072 | bytes 1589248 | tf_op jit(solution)/shard_map/scatter-add | solution.py:22
  50.8 31.4 %all-gather = f32[256,512]{1,0:T(8,128)S(1)} all-gather(f32[32,512]{1,0:T(8,128)S(1)} %fusion.54), channel_id=2, replica_groups=mesh['front'=4,'row'=8] {'row'}, dimensions={0}, use_global_device_ids=true | all-gather | bytes 589824 | tf_op jit(solution)/shard_map/all_gather | solution.py:40
  82.3 2.3 %fusion.41 = f32[32,512]{1,0:T(8,128)S(1)} fusion(f32[32,512]{1,0:T(8,128)S(1)} %reduce_sum.36, f32[1,4,512,512]{3,2,1,0:T(8,128)} %param.12), kind=kOutput, calls=%fused_computation.27 | convolution fusion | flops 100663296 | bytes 1179648 | tf_op jit(solution)/shard_map/dot_general | solution.py:41
  84.6 1.6 convolution_subtract_fusion.2
  86.6 31.3 %all-gather.1 = f32[256,512]{1,0:T(8,128)S(1)} all-gather(f32[32,512]{1,0:T(8,128)S(1)} %fusion.56), channel_id=3, replica_groups=mesh['front'=4,'row'=8] {'row'}, dimensions={0}, use_global_device_ids=true | all-gather | bytes 589824 | tf_op jit(solution)/shard_map/all_gather | solution.py:40
  117.9 2.3 %fusion.39 = f32[32,512]{1,0:T(8,128)S(1)} fusion(f32[32,512]{1,0:T(8,128)S(1)} %reduce_sum.37, f32[1,4,512,512]{3,2,1,0:T(8,128)} %param.12), kind=kOutput, calls=%fused_computation.25 | convolution fusion | flops 100663296 | bytes 1179648 | tf_op jit(solution)/shard_map/dot_general | solution.py:41
  120.2 1.6 convolution_subtract_fusion.1
  122.2 31.3 %all-gather.2 = f32[256,512]{1,0:T(8,128)S(1)} all-gather(f32[32,512]{1,0:T(8,128)S(1)} %fusion.58), channel_id=4, replica_groups=mesh['front'=4,'row'=8] {'row'}, dimensions={0}, use_global_device_ids=true | all-gather | bytes 589824 | tf_op jit(solution)/shard_map/all_gather | solution.py:40
  153.5 2.3 %fusion.37 = f32[32,512]{1,0:T(8,128)S(1)} fusion(f32[32,512]{1,0:T(8,128)S(1)} %reduce_sum.38, f32[1,4,512,512]{3,2,1,0:T(8,128)} %param.12), kind=kOutput, calls=%fused_computation.23 | convolution fusion | flops 100663296 | bytes 1179648 | tf_op jit(solution)/shard_map/dot_general | solution.py:41
  155.8 1.6 convolution_subtract_fusion
  157.8 31.4 %all-gather.3 = f32[256,512]{1,0:T(8,128)S(1)} all-gather(f32[32,512]{1,0:T(8,128)S(1)} %fusion.60), channel_id=5, replica_groups=mesh['front'=4,'row'=8] {'row'}, dimensions={0}, use_global_device_ids=true | all-gather | bytes 589824 | tf_op jit(solution)/shard_map/all_gather | solution.py:40
  189.2 2.3 %fusion.35 = f32[32,512]{1,0:T(8,128)S(1)} fusion(f32[32,512]{1,0:T(8,128)S(1)} %reduce_sum.39, f32[1,4,512,512]{3,2,1,0:T(8,128)} %param.12), kind=kOutput, calls=%fused_computation.21 | convolution fusion | flops 100663296 | bytes 1179648 | tf_op jit(solution)/shard_map/dot_general | solution.py:41
  191.5 4.8 %fusion.26 = f32[32,1536]{1,0:T(8,128)S(1)} fusion(f32[32,512]{1,0:T(8,128)S(1)} %fusion.37, f32[1536,2048]{1,0:T(8,128)} %bitcast.66, f32[1536]{0:T(1024)S(1)} %copy-done.3), kind=kOutput, calls=%fused_computation.15 | convolution fusion | flops 302039040 | bytes 3414016 | tf_op jit(solution)/shard_map/dot_general | solution.py:56
  196.3 4.8 %fusion.23 = f32[32,1536]{1,0:T(8,128)S(1)} fusion(f32[32,512]{1,0:T(8,128)S(1)} %fusion.39, f32[1536,2048]{1,0:T(8,128)} %bitcast.67, f32[1536]{0:T(1024)S(1)} %copy-done.1), kind=kOutput, calls=%fused_computation.14 | convolution fusion | flops 302039040 | bytes 3414016 | tf_op jit(solution)/shard_map/dot_general | solution.py:56
  201.4 4.8 %fusion.29 = f32[32,1536]{1,0:T(8,128)S(1)} fusion(f32[32,512]{1,0:T(8,128)S(1)} %fusion.35, f32[1536,2048]{1,0:T(8,128)} %bitcast.68, f32[1536]{0:T(1024)S(1)} %copy-done.2), kind=kOutput, calls=%fused_computation.16 | convolution fusion | flops 302039040 | bytes 3414016 | tf_op jit(solution)/shard_map/dot_general | solution.py:56
  206.2 0.6 fusion.73
  206.8 5.5 %fusion.32 = f32[1,32,1536]{2,1,0:T(8,128)} fusion(f32[32,1536]{1,0:T(8,128)S(1)} %fusion.29, f32[32,1536]{1,0:T(8,128)S(1)} %fusion.26, f32[32,1536]{1,0:T(8,128)S(1)} %fusion.23, f32[32,1536]{1,0:T(8,128)S(1)} %copy.26, f32[32,512]{1,0:T(8,128)S(1)} %fusion.41, f32[1536,2048]{1,0:T(8,128)} %bitcast.69, f32[1536]{0:T(1024)S(1)} %copy-done), kind=kOutput, calls=%fused_computation.17 | convolution fusion | flops 302235648 | bytes 4200448 | tf_op jit(solution)/shard_map/dot_general | solution.py:56
  (34 shorter events, 2.9 us)
Async XLA Ops:
  2.8 23.6 %all-to-all-start = ((f32[32,1,32,128]{3,0,1,2:T(8,128)}), f32[32,1,32,128]{3,0,1,2:T(8,128)S(1)}, u32[]{:S(2)}, u32[]{:S(2)}) async-start(f32[32,1,32,128]{3,0,1,2:T(8,128)} %bitcast.4), calls=%async_computation | async-start | bytes 1048576 | tf_op jit(solution)/shard_map/all_to_all | solution.py:18
  27.6 22.8 %copy-start.4 = (s32[256]{0:T(256)S(1)}, s32[256]{0:T(256)}, u32[]{:S(2)}) copy-start(s32[256]{0:T(256)} %and_select_fusion) | copy-start | bytes 3076
  27.6 22.8 %copy-start.8 = (pred[256]{0:T(512)(128)(4,1)S(1)}, pred[256]{0:T(512)(128)(4,1)}, u32[]{:S(2)}) copy-start(pred[256]{0:T(512)(128)(4,1)} %broadcast_compare_fusion.2) | copy-start | bytes 772
  50.3 35.9 %copy-start.6 = (pred[256]{0:T(512)(128)(4,1)S(1)}, pred[256]{0:T(512)(128)(4,1)}, u32[]{:S(2)}) copy-start(pred[256]{0:T(512)(128)(4,1)} %broadcast_compare_fusion.4) | copy-start | bytes 772
  50.3 71.5 %copy-start.5 = (pred[256]{0:T(512)(128)(4,1)S(1)}, pred[256]{0:T(512)(128)(4,1)}, u32[]{:S(2)}) copy-start(pred[256]{0:T(512)(128)(4,1)} %broadcast_compare_fusion.1) | copy-start | bytes 772
  82.3 75.1 %copy-start.7 = (pred[256]{0:T(512)(128)(4,1)S(1)}, pred[256]{0:T(512)(128)(4,1)}, u32[]{:S(2)}) copy-start(pred[256]{0:T(512)(128)(4,1)} %broadcast_compare_fusion) | copy-start | bytes 772
  117.9 73.6 %copy-start.3 = (f32[1536]{0:T(1024)S(1)}, f32[1536]{0:T(1024)}, u32[]{:S(2)}) copy-start(f32[1536]{0:T(1024)} %get-tuple-element.7) | copy-start | bytes 18436
  153.5 42.8 %copy-start.1 = (f32[1536]{0:T(1024)S(1)}, f32[1536]{0:T(1024)}, u32[]{:S(2)}) copy-start(f32[1536]{0:T(1024)} %broadcast_bitcast_fusion.2) | copy-start | bytes 18436
  191.5 9.9 %copy-start.2 = (f32[1536]{0:T(1024)S(1)}, f32[1536]{0:T(1024)}, u32[]{:S(2)}) copy-start(f32[1536]{0:T(1024)} %get-tuple-element.6) | copy-start | bytes 18436
  196.3 10.5 %copy-start = (f32[1536]{0:T(1024)S(1)}, f32[1536]{0:T(1024)}, u32[]{:S(2)}) copy-start(f32[1536]{0:T(1024)} %broadcast_bitcast_fusion.3) | copy-start | bytes 18436
